TPU v7x, 256 devices: a whole 4x4x8 slice. The times are simulated.
256 devices in a mesh: row: 16 (over y, x), proto: 16 (over z, core).
Axes of the slice: x: 4, y: 4, z: 8, core: 2. Of those that a mesh axis runs over, the one named last changes fastest.
Arguments:
- embeddings: bfloat16 [32768, 1024], P('row'), may hold values from -24 to 24, as said below
- prototypes: bfloat16 [16384, 1024], P('proto', 'row'), may hold values from -6 to 6
- block_mask: int32 [256, 128], P('row', 'proto'), may hold values from 0 to 1, as said below
Outputs:
- targets: bfloat16 [32768, 1024], P('row', 'proto')
- row_potential: float32 [32768], P('row')
- column_potential: float32 [16384], P('proto')
Inputs may be any that keep to these rules, and one draw needn't show every extreme that they name: `block_mask`: every row tile and every prototype tile has at least one candidate tile. `embeddings`: some rows copy a scaled prototype.
All inputs are finite; a program needn't handle non-finite values.
Results may differ from a plain program's by a relative error of at most 0.02.
Values may be sent and summed in bfloat16 or wider, within the bound.
A program may use at most 64 MiB of HBM per device.

v0:
```python
import math

import jax
import jax.numpy as jnp
from jax import lax
from jax.sharding import PartitionSpec as P

ITERS = 3


NEGATIVE = -1e30


def expand_mask(block_mask, tile):
    allowed = block_mask == 1
    return jnp.repeat(jnp.repeat(allowed, tile, axis=0), tile, axis=1)


def row_logsum(values, allowed):
    peak = lax.pmax(jnp.max(jnp.where(allowed, values, NEGATIVE), axis=1), "proto")
    total = lax.psum(
        jnp.sum(jnp.where(allowed, jnp.exp(values - peak[:, None]), 0.0), axis=1), "proto"
    )
    return peak + jnp.log(total)


def column_logsum(values, allowed):
    peak = lax.pmax(jnp.max(jnp.where(allowed, values, NEGATIVE), axis=0), "row")
    total = lax.psum(
        jnp.sum(jnp.where(allowed, jnp.exp(values - peak[None, :]), 0.0), axis=0), "row"
    )
    return peak + jnp.log(total)


def shards(embeddings, prototypes, block_mask):
    features = lax.all_gather(prototypes, "row", axis=1, tiled=True)
    scale = 4.0 / math.sqrt(features.shape[1])
    similar = (
        lax.dot_general(
            embeddings, features, (((1,), (1,)), ((), ())), preferred_element_type=jnp.float32
        )
        * scale
    )
    tile = similar.shape[0] // block_mask.shape[0]
    allowed = expand_mask(block_mask, tile)
    rows_all = similar.shape[0] * lax.axis_size("row")
    protos_all = similar.shape[1] * lax.axis_size("proto")
    log_column = math.log(rows_all / protos_all)
    column_potential = jnp.zeros((similar.shape[1],), jnp.float32)
    row_potential = jnp.zeros((similar.shape[0],), jnp.float32)
    for sweep in range(ITERS):
        row_potential = -row_logsum(similar + column_potential[None, :], allowed)
        column_potential = log_column - column_logsum(similar + row_potential[:, None], allowed)
    plan = jnp.where(
        allowed, jnp.exp(similar + row_potential[:, None] + column_potential[None, :]), 0.0
    ).astype(jnp.bfloat16)
    partial_value = jnp.dot(plan, features, preferred_element_type=jnp.float32)
    targets = lax.psum_scatter(
        partial_value.astype(jnp.bfloat16), "proto", scatter_dimension=1, tiled=True
    )
    return (targets, row_potential, column_potential)


def solution(mesh):
    return jax.shard_map(
        shards,
        mesh=mesh,
        in_specs=(P("row", None), P("proto", "row"), P("row", "proto")),
        out_specs=(P("row", "proto"), P("row"), P("proto")),
        check_vma=False,
    )
```

profile of v0, /device:TPU:1, one launch (start us, length us, event | category | flops | bytes accessed | tf_op | source)
XLA Modules:
  0.0 572.9 jit_solution(16781817133528118072)
XLA Ops:
  8.7 54.6 %all-gather.2.cloned.1.call-done = bf16[1024,1024]{0,1:T(8,128)(2,1)} async-done(((bf16[1024,64]{0,1:T(8,128)(2,1)}), bf16[1024,1024]{0,1:T(8,128)(2,1)}) %all-gather.2.cloned.1.call-update) | async-done | bytes 2097168 | tf_op jit(solution)/shard_map/all_gather | solution.py:36
  63.5 6.4 %broadcast_in_dim.38 = pred[2048,8,128]{2,1,0:T(8,128)(4,1)S(1)} broadcast(pred[2048,8]{1,0:T(8,128)(4,1)S(1)} %bitcast.35), dimensions={0,1} | broadcast | bytes 2113536 | tf_op jit(solution)/shard_map/broadcast_in_dim | solution.py:16
  69.8 11.4 %select_reduce_fusion.11 = (f32[2048]{0:T(1024)S(1)}, f32[2048,1024]{1,0:T(8,128)}) fusion(pred[256,8,8,128]{3,2,1,0:T(8,128)(4,1)S(1)} %bitcast.22, bf16[2048,1024]{1,0:T(8,128)(2,1)} %param.3, bf16[1024,1024]{0,1:T(8,128)(2,1)} %all-gather.2.cloned.1.call-done), kind=kOutput, calls=%fused_computation.12 | convolution fusion | flops 4301256704 | bytes 16785408 | tf_op jit(solution)/shard_map/dot_general | solution.py:39
  81.2 25.3 %pmax.42 = f32[2048]{0:T(1024)S(1)} all-reduce(f32[2048]{0:T(1024)S(1)} %get-tuple-element.3), channel_id=1, replica_groups=mesh['row'=16,'proto'=16] {'proto'}, use_global_device_ids=true, to_apply=%region_1.2 | all-reduce | flops 2048 | bytes 16384 | tf_op jit(solution)/shard_map/pmax | solution.py:20
  111.2 25.5 %psum.42 = f32[2048]{0:T(1024)S(1)} all-reduce(f32[2048]{0:T(1024)S(1)} %select_reduce_fusion.10), channel_id=1, replica_groups=mesh['row'=16,'proto'=16] {'proto'}, use_global_device_ids=true, to_apply=%region_3.4 | all-reduce | flops 2048 | bytes 16384 | tf_op jit(solution)/shard_map/psum | solution.py:21
  141.0 30.9 %pmax.43 = f32[1024]{0:T(1024)S(1)} all-reduce(f32[1024]{0:T(1024)S(1)} %select_reduce_fusion.9), channel_id=1, replica_groups=mesh['row'=16,'proto'=16] {'row'}, use_global_device_ids=true, to_apply=%region_5.6 | all-reduce | flops 1024 | bytes 8192 | tf_op jit(solution)/shard_map/pmax | solution.py:28
  171.9 4.7 select_reduce_fusion.8
  176.6 28.5 %psum.43 = f32[1024]{0:T(1024)S(1)} all-reduce(f32[1024]{0:T(1024)S(1)} %select_reduce_fusion.8), channel_id=1, replica_groups=mesh['row'=16,'proto'=16] {'row'}, use_global_device_ids=true, to_apply=%region_7.8 | all-reduce | flops 1024 | bytes 8192 | tf_op jit(solution)/shard_map/psum | solution.py:29
  205.1 5.0 select_reduce_fusion.7
  210.1 38.4 %pmax.44 = f32[2048]{0:T(1024)S(1)} all-reduce(f32[2048]{0:T(1024)S(1)} %select_reduce_fusion.7), channel_id=1, replica_groups=mesh['row'=16,'proto'=16] {'proto'}, use_global_device_ids=true, to_apply=%region_9.10 | all-reduce | flops 2048 | bytes 16384 | tf_op jit(solution)/shard_map/pmax | solution.py:20
  248.5 4.8 select_reduce_fusion.6
  253.3 24.1 %psum.44 = f32[2048]{0:T(1024)S(1)} all-reduce(f32[2048]{0:T(1024)S(1)} %select_reduce_fusion.6), channel_id=1, replica_groups=mesh['row'=16,'proto'=16] {'proto'}, use_global_device_ids=true, to_apply=%region_11.12 | all-reduce | flops 2048 | bytes 16384 | tf_op jit(solution)/shard_map/psum | solution.py:21
  281.7 30.2 %pmax.45 = f32[1024]{0:T(1024)S(1)} all-reduce(f32[1024]{0:T(1024)S(1)} %select_reduce_fusion.5), channel_id=1, replica_groups=mesh['row'=16,'proto'=16] {'row'}, use_global_device_ids=true, to_apply=%region_13.14 | all-reduce | flops 1024 | bytes 8192 | tf_op jit(solution)/shard_map/pmax | solution.py:28
  311.9 4.7 select_reduce_fusion.4
  316.6 28.5 %psum.45 = f32[1024]{0:T(1024)S(1)} all-reduce(f32[1024]{0:T(1024)S(1)} %select_reduce_fusion.4), channel_id=1, replica_groups=mesh['row'=16,'proto'=16] {'row'}, use_global_device_ids=true, to_apply=%region_15.16 | all-reduce | flops 1024 | bytes 8192 | tf_op jit(solution)/shard_map/psum | solution.py:29
  345.1 5.0 select_reduce_fusion.3
  350.1 38.2 %pmax.46 = f32[2048]{0:T(1024)S(1)} all-reduce(f32[2048]{0:T(1024)S(1)} %select_reduce_fusion.3), channel_id=1, replica_groups=mesh['row'=16,'proto'=16] {'proto'}, use_global_device_ids=true, to_apply=%region_17.18 | all-reduce | flops 2048 | bytes 16384 | tf_op jit(solution)/shard_map/pmax | solution.py:20
  388.4 4.8 select_reduce_fusion.2
  393.2 24.1 %psum.46 = f32[2048]{0:T(1024)S(1)} all-reduce(f32[2048]{0:T(1024)S(1)} %select_reduce_fusion.2), channel_id=1, replica_groups=mesh['row'=16,'proto'=16] {'proto'}, use_global_device_ids=true, to_apply=%region_19.20 | all-reduce | flops 2048 | bytes 16384 | tf_op jit(solution)/shard_map/psum | solution.py:21
  421.5 30.2 %pmax.47 = f32[1024]{0:T(1024)S(1)} all-reduce(f32[1024]{0:T(1024)S(1)} %select_reduce_fusion.1), channel_id=1, replica_groups=mesh['row'=16,'proto'=16] {'row'}, use_global_device_ids=true, to_apply=%region_21.22 | all-reduce | flops 1024 | bytes 8192 | tf_op jit(solution)/shard_map/pmax | solution.py:28
  451.8 4.7 select_reduce_fusion
  456.5 28.7 %psum.47 = f32[1024]{0:T(1024)S(1)} all-reduce(f32[1024]{0:T(1024)S(1)} %select_reduce_fusion), channel_id=1, replica_groups=mesh['row'=16,'proto'=16] {'row'}, use_global_device_ids=true, to_apply=%region_23.24 | all-reduce | flops 1024 | bytes 8192 | tf_op jit(solution)/shard_map/psum | solution.py:29
  485.2 10.8 %fusion.4 = bf16[2048,1024]{0,1:T(8,128)(2,1)} fusion(bf16[1024,1024]{0,1:T(8,128)(2,1)} %all-gather.2.cloned.1.call-done, f32[2048,1024]{1,0:T(8,128)} %get-tuple-element.4, f32[1024]{0:T(1024)S(1)} %add_subtract_fusion, f32[2048]{0:T(1024)S(1)} %add_negate_fusion, pred[256,8,8,128]{3,2,1,0:T(8,128)(4,1)S(1)} %bitcast.34), kind=kOutput, calls=%fused_computation.18 | convolution fusion | flops 4305453056 | bytes 16789504 | tf_op jit(solution)/shard_map/dot_general | solution.py:57
  496.1 69.9 %reduce-scatter.2.cloned.1.call-done = bf16[2048,64]{0,1:T(8,128)(2,1)} async-done(((bf16[2048,1024]{0,1:T(8,128)(2,1)}), bf16[2048,64]{0,1:T(8,128)(2,1)}) %reduce-scatter.2.cloned.1.call-update) | async-done | bytes 262160 | tf_op jit(solution)/shard_map/reduce_scatter | solution.py:58
  (21 shorter events, 19.2 us)
Async XLA Ops:
  7.2 56.2 %all-gather.2.cloned.1.call-start = ((), (), s32[]{:S(2)}) async-start(), calls=%async_computation.1 | async-start | bytes 2228224 | tf_op jit(solution)/shard_map/all_gather | solution.py:36
  7.9 558.1 %reduce-scatter.2.cloned.1.call-start = ((), (), s32[]{:S(2)}) async-start(), calls=%async_computation.2 | async-start | bytes 4456448 | tf_op jit(solution)/shard_map/reduce_scatter | solution.py:58
  417.2 68.0 %copy-start = (f32[2048]{0:T(1024)}, f32[2048]{0:T(1024)S(1)}, u32[]{:S(2)}) copy-start(f32[2048]{0:T(1024)S(1)} %add_negate_fusion) | copy-start | bytes 24580
  485.2 10.9 %copy-start.1 = (f32[1024]{0:T(1024)}, f32[1024]{0:T(1024)S(1)}, u32[]{:S(2)}) copy-start(f32[1024]{0:T(1024)S(1)} %add_subtract_fusion) | copy-start | bytes 12292
Sparse Core Ops, SparseCore 0:
  10.4 52.8 all-gather.1
  496.2 69.7 reduce-scatter.1
where the time goes:
time: 576 us; the launch traced here: 573 us
  blocking collectives  353 us (61%)
  waiting for transfers between devices  125 us (22%)
  other arithmetic  51.8 us (9%)
  matrix products  22.2 us (4%)
  between operations  14.2 us (2%)
  local copies, waits for them, and re-layouts  6.54 us (1%)
    pmax x3, blocking collectives, row_logsum(): lax.pmax(jnp.max(jnp.where(allowed, values, NEGATIVE), axis=1), 'proto')  102 us
    pmax x3, blocking collectives, column_logsum(): lax.pmax(jnp.max(jnp.where(allowed, values, NEGATIVE), axis=0), 'row')  91.4 us
    psum x3, blocking collectives, column_logsum(): lax.psum(jnp.sum(jnp.where(allowed, jnp.exp(values - peak[None, :]), 0.0)...  85.7 us
    psum x3, blocking collectives, row_logsum(): lax.psum(jnp.sum(jnp.where(allowed, jnp.exp(values - peak[:, None]), 0.0)...  73.6 us
    reduce_scatter x1, waiting for transfers between devices, shards(): lax.psum_scatter(partial_value.astype(jnp.bfloat16), 'proto', scatter_dim...  69.9 us
    all_gather x1, waiting for transfers between devices, shards(): features = lax.all_gather(prototypes, 'row', axis=1, tiled=True)  54.6 us
    reduce_sum x3, other arithmetic, row_logsum(): jnp.sum(jnp.where(allowed, jnp.exp(values - peak[:, None]), 0.0), axis=1)  14.3 us
    reduce_sum x3, other arithmetic, column_logsum(): jnp.sum(jnp.where(allowed, jnp.exp(values - peak[None, :]), 0.0), axis=0)  14.1 us
  transfers between devices with their start and end apart: 2, of which 2 were waited for; matrix products, arithmetic and copies ran while one was open for 0% of the time, Pallas kernels for 0%

commit v1 on v0

v1 whole, which is shorter than its diff:
```python
import functools
import math

import jax
import jax.numpy as jnp
from jax import lax
from jax.experimental import pallas as pl
from jax.experimental.pallas import tpu as pltpu
from jax.sharding import PartitionSpec as P

ITERS = 3
TILE = 128
NEGATIVE = -1e30
LOWEST = -1e38
LOG2E = 1.4426950408889634
LN2 = 0.6931471805599453
MESH = pl.DeviceIdType.MESH


def tree_reduce(op, parts):
    while len(parts) > 1:
        pairs = [op(parts[i], parts[i + 1]) for i in range(0, len(parts) - 1, 2)]
        parts = pairs + ([parts[-1]] if len(parts) % 2 else [])
    return parts[0]


def kernel(
    cfg,
    own_ref,
    emb_hbm,
    mask_ref,
    out_ref,
    row_out,
    col_out,
    emb,
    feat,
    sim,
    wide,
    row_send,
    row_recv,
    col_send,
    col_recv,
    part,
    sib_recv,
    tx,
    rx,
    emb_sem,
    gs_sem,
    gr_sem,
    rs_sem,
    rr_sem,
    cs_sem,
    cr_sem,
    ss_sem,
    sr_sem,
    ts_sem,
    tr_sem,
):
    side, n_row, n_proto, log_column = cfg
    n_z = n_proto // 2
    slab, protos = own_ref.shape
    share = out_ref.shape[0]
    depth = feat.shape[0]
    rows = sim.shape[0]
    row_tiles, col_tiles = rows // TILE, protos // TILE
    scale = 4.0 / math.sqrt(depth) * LOG2E

    r = lax.axis_index("row")
    p = lax.axis_index("proto")
    y, x = r // side, lax.rem(r, side)
    z, c = p // 2, lax.rem(p, 2)

    def row_of(dy, dx):
        return lax.rem(y + dy + 2 * side, side) * side + lax.rem(x + dx + 2 * side, side)

    emb_copy = pltpu.make_async_copy(emb_hbm, emb, emb_sem)
    emb_copy.start()

    barrier = pltpu.get_barrier_semaphore()
    for d in range(1, n_row):
        pl.semaphore_signal(
            barrier, inc=1, device_id=(lax.rem(r + d, n_row), p), device_id_type=MESH
        )
    for d in range(1, n_proto):
        pl.semaphore_signal(
            barrier, inc=1, device_id=(r, lax.rem(p + d, n_proto)), device_id_type=MESH
        )
    pl.semaphore_wait(barrier, n_row + n_proto - 2)

    half, quarter = slab // 2, slab // 4

    def shift(tree, df, ds):
        return (ds, df) if tree == 0 else (df, ds)

    def piece(tree, df, ds, which, ref=None):
        start = tree * half + (quarter if which == "hi" else 0)
        size = half if which == "all" else quarter
        if ref is not None:
            return ref.at[pl.ds(start, size), :]
        return feat.at[pl.ds(pl.multiple_of(row_of(*shift(tree, df, ds)) * slab + start, quarter), size), :]

    moves = {}

    def gather_copy(tree, key, src_at, move, which, from_own):
        slot = moves.setdefault((tree, key), len([k for k in moves if k[0] == tree]))
        block = piece(tree, *src_at, which)
        src = piece(tree, 0, 0, which, own_ref) if from_own else block
        return pltpu.make_async_remote_copy(
            src_ref=src,
            dst_ref=block,
            send_sem=gs_sem.at[tree, slot],
            recv_sem=gr_sem.at[tree, slot],
            device_id=(row_of(*shift(tree, *move)), p),
            device_id_type=MESH,
        )

    sent = []

    def push(tree, key, src_at, move, which, from_own=False):
        copy = gather_copy(tree, key, src_at, move, which, from_own)
        copy.start()
        sent.append(copy)

    if n_row > 1:
        trees = (0, 1)
        for t in trees:
            push(t, "f+", (0, 0), (1, 0), "all", True)
            push(t, "f-", (0, 0), (-1, 0), "all", True)
        for t in trees:
            push(t, "s+0", (0, 0), (0, 1), "all", True)
            push(t, "s-0", (0, 0), (0, -1), "all", True)

    feat[pl.ds(pl.multiple_of(r * slab, slab), slab), :] = own_ref[...]

    if n_row > 1:

        def across(t, df):
            push(t, "s+%d" % df, (df, 0), (0, 1), "all")
            push(t, "s-%d" % df, (df, 0), (0, -1), "all")

        def relay(t, df):
            arrive(t, "s+%d" % df, (df, -1), (0, 1))
            push(t, "t+%d" % df, (df, -1), (0, 1), "lo")
            arrive(t, "s-%d" % df, (df, 1), (0, -1))
            push(t, "t-%d" % df, (df, 1), (0, -1), "hi")

        def arrive(t, key, at, move, which="all"):
            slot = moves[(t, key)]
            block = piece(t, *at, which)
            pltpu.make_async_remote_copy(
                src_ref=block,
                dst_ref=block,
                send_sem=gs_sem.at[t, slot],
                recv_sem=gr_sem.at[t, slot],
                device_id=(row_of(*shift(t, *move)), p),
                device_id_type=MESH,
            ).wait_recv()

        for t in trees:
            arrive(t, "f+", (-1, 0), (1, 0))
            push(t, "g+", (-1, 0), (1, 0), "lo")
            arrive(t, "f-", (1, 0), (-1, 0))
            push(t, "g-", (1, 0), (-1, 0), "hi")
        for t in trees:
            across(t, -1)
            across(t, 1)
        for t in trees:
            relay(t, 0)
        for t in trees:
            arrive(t, "g+", (2, 0), (1, 0), "lo")
            arrive(t, "g-", (2, 0), (-1, 0), "hi")
            across(t, 2)
        for t in trees:
            relay(t, -1)
            relay(t, 1)
        for t in trees:
            relay(t, 2)
        for t in trees:
            for df in (0, -1, 1, 2):
                arrive(t, "t+%d" % df, (df, 2), (0, 1), "lo")
                arrive(t, "t-%d" % df, (df, 2), (0, -1), "hi")

    emb_copy.wait()

    mm, mn = min(512, rows), min(256, protos)

    def score_block(step, carry):
        i, j = step // (protos // mn), lax.rem(step, protos // mn)
        row0 = pl.multiple_of(i * mm, mm)
        col0 = pl.multiple_of(j * mn, mn)
        acc = jnp.dot(
            emb[pl.ds(row0, mm), :], feat[:, pl.ds(col0, mn)], preferred_element_type=jnp.float32
        )
        for a in range(mm // TILE):
            for b in range(mn // TILE):
                allowed = mask_ref[i * (mm // TILE) + a, j * (mn // TILE) + b] == 1
                bias = jnp.where(allowed, 0.0, NEGATIVE)
                sim[
                    pl.ds(pl.multiple_of(row0 + a * TILE, TILE), TILE),
                    pl.ds(pl.multiple_of(col0 + b * TILE, TILE), TILE),
                ] = acc[a * TILE : (a + 1) * TILE, b * TILE : (b + 1) * TILE] * scale + bias
        return carry

    lax.fori_loop(0, (rows // mm) * (protos // mn), score_block, 0)

    group = 16

    def row_partial(shifts):
        def block(step, carry):
            base = pl.multiple_of(step * group, group)
            vals = []
            for j in range(col_tiles):
                v = sim[pl.ds(base, group), j * TILE : (j + 1) * TILE]
                if shifts is not None:
                    v = v + shifts[j : j + 1, :]
                vals.append(v)
            peak = tree_reduce(jnp.maximum, vals)
            total = tree_reduce(jnp.add, [jnp.exp2(v - peak) for v in vals])
            wide[pl.ds(base, group), :] = peak + jnp.log2(total)
            return carry

        lax.fori_loop(0, rows // group, block, 0, unroll=2)

    def row_finish(k):
        def block(i, carry):
            t = jnp.transpose(wide[pl.ds(pl.multiple_of(i * TILE, TILE), TILE), :])
            peak = jnp.max(t, axis=0, keepdims=True)
            total = jnp.sum(jnp.exp2(t - peak), axis=0, keepdims=True)
            row_send[k, pl.ds(i, 1), :] = peak + jnp.log2(total)
            return carry

        lax.fori_loop(0, row_tiles, block, 0, unroll=4)

    def exchange(send, recv, send_sem, recv_sem, k, n, target):
        for d in range(1, n):
            pltpu.make_async_remote_copy(
                src_ref=send.at[k],
                dst_ref=recv.at[k, d - 1],
                send_sem=send_sem.at[k],
                recv_sem=recv_sem.at[k],
                device_id=target(d),
                device_id_type=MESH,
            ).start()
        if n > 1:
            pltpu.make_async_remote_copy(
                src_ref=recv.at[k],
                dst_ref=recv.at[k],
                send_sem=send_sem.at[k],
                recv_sem=recv_sem.at[k],
                device_id=target(1),
                device_id_type=MESH,
            ).wait()
        parts = [send[k]] + [recv[k, d - 1] for d in range(1, n)]
        peak = tree_reduce(jnp.maximum, parts)
        total = tree_reduce(jnp.add, [jnp.exp2(v - peak) for v in parts])
        return peak + jnp.log2(total)

    def spread_rows():
        def block(i, carry):
            u = jnp.broadcast_to(row_out[pl.ds(i, 1), :], (TILE, TILE))
            wide[pl.ds(pl.multiple_of(i * TILE, TILE), TILE), :] = jnp.transpose(u)
            return carry

        lax.fori_loop(0, row_tiles, block, 0, unroll=4)

    def column_partial(k):
        def block(i, carry):
            base = pl.multiple_of(i * TILE, TILE)
            out = []
            for j in range(col_tiles):
                top, total = carry[j]
                v = sim[pl.ds(base, TILE), j * TILE : (j + 1) * TILE] + wide[pl.ds(base, TILE), :]
                v = v.reshape(TILE // 8, 8, TILE)
                new = jnp.maximum(top, tree_reduce(jnp.maximum, [v[g] for g in range(TILE // 8)]))
                add = tree_reduce(jnp.add, [jnp.exp2(v[g] - new) for g in range(TILE // 8)])
                out.append((new, total * jnp.exp2(top - new) + add))
            return tuple(out)

        start = tuple(
            (jnp.full((8, TILE), LOWEST, jnp.float32), jnp.zeros((8, TILE), jnp.float32))
            for _ in range(col_tiles)
        )
        done = lax.fori_loop(0, row_tiles, block, start)
        for j in range(col_tiles):
            level = done[j][0] + jnp.log2(done[j][1])
            peak = jnp.max(level, axis=0, keepdims=True)
            total = jnp.sum(jnp.exp2(level - peak), axis=0, keepdims=True)
            col_send[k, j : j + 1, :] = peak + jnp.log2(total)

    shifts = None
    for k in range(ITERS):
        row_partial(shifts)
        row_finish(k)
        row_out[...] = -exchange(
            row_send, row_recv, rs_sem, rr_sem, k, n_proto, lambda d: (r, lax.rem(p + d, n_proto))
        )
        spread_rows()
        column_partial(k)
        shifts = log_column - exchange(
            col_send, col_recv, cs_sem, cr_sem, k, n_row, lambda d: (lax.rem(r + d, n_row), p)
        )

    col_out[...] = shifts * LN2

    plan = emb

    def plan_block(step, carry):
        base = pl.multiple_of(step * group, group)
        u = wide[pl.ds(base, group), :]
        for j in range(col_tiles):
            v = sim[pl.ds(base, group), j * TILE : (j + 1) * TILE] + (u + shifts[j : j + 1, :])
            plan[pl.ds(base, group), j * TILE : (j + 1) * TILE] = jnp.exp2(v).astype(jnp.bfloat16)
        return carry

    lax.fori_loop(0, rows // group, plan_block, 0, unroll=2)
    row_out[...] = row_out[...] * LN2

    width = rows // 2
    tn = min(256, rows)

    def product(t):
        feat0 = pl.multiple_of(lax.rem(z + t, n_z) * 2 * share, 2 * share)

        def block(n, carry):
            row0 = pl.multiple_of(n * tn, tn)
            part[t, :, pl.ds(row0, tn)] = lax.dot_general(
                feat[pl.ds(feat0, 2 * share), :],
                plan[pl.ds(row0, tn), :],
                (((1,), (1,)), ((), ())),
                preferred_element_type=jnp.float32,
            ).astype(jnp.bfloat16)
            return carry

        lax.fori_loop(0, rows // tn, block, 0)

    def sibling_copy(t):
        other = 1 - c
        return pltpu.make_async_remote_copy(
            src_ref=part.at[t, pl.ds(pl.multiple_of(other * share, share), share), :],
            dst_ref=sib_recv.at[t],
            send_sem=ss_sem.at[t],
            recv_sem=sr_sem.at[t],
            device_id=(r, z * 2 + other),
            device_id_type=MESH,
        )

    def chip_sum(t, h):
        mine = part[t, pl.ds(pl.multiple_of(c * share, share), share), h * width : (h + 1) * width]
        theirs = sib_recv[t, :, h * width : (h + 1) * width]
        return mine.astype(jnp.float32) + theirs.astype(jnp.float32)

    def chain_copy(way, d, h):
        step = 1 if way == 0 else n_z - 1
        return pltpu.make_async_remote_copy(
            src_ref=tx.at[way, d - 1, h],
            dst_ref=rx.at[way, d - 1, h],
            send_sem=ts_sem.at[way, d - 1, h],
            recv_sem=tr_sem.at[way, d - 1, h],
            device_id=(r, lax.rem(z + step, n_z) * 2 + c),
            device_id_type=MESH,
        )

    far = n_z // 2
    flying = []

    def forward(way, d, h):
        t = d if way == 0 else n_z - d
        value = chip_sum(t, h)
        if d < far and (d + 1 < far or h == way):
            chain_copy(way, d + 1, h).wait_recv()
            value = value + rx[way, d, h].astype(jnp.float32)
        tx[way, d - 1, h] = value.astype(jnp.bfloat16)
        copy = chain_copy(way, d, h)
        copy.start()
        flying.append(copy)

    def ready(t):
        product(t)
        copy = sibling_copy(t)
        copy.start()
        return copy

    waiting = {}
    order = [far] + [t for d in range(far - 1, 0, -1) for t in (d, n_z - d)] + [0] if far else [0]
    for t in order[:3]:
        waiting[t] = ready(t)
    if far:
        waiting[far].wait()
        forward(0, far, 0)
        forward(1, far, 1)
    done = 3
    for d in range(far - 1, 0, -1):
        for t in (d, n_z - d):
            waiting[t].wait()
        forward(0, d, 1)
        forward(1, d, 0)
        for t in order[done : done + 2]:
            waiting[t] = ready(t)
        done += 2
        forward(0, d, 0)
        forward(1, d, 1)
    for t in order[done:]:
        waiting[t] = ready(t)
    waiting[0].wait()
    for h in (1, 0):
        value = chip_sum(0, h)
        for way in (0, 1):
            if far > 1 or (far == 1 and h == way):
                chain_copy(way, 1, h).wait_recv()
                value = value + rx[way, 0, h].astype(jnp.float32)
        out_ref[:, h * width : (h + 1) * width] = value.astype(jnp.bfloat16)

    for copy in sent + flying:
        copy.wait_send()


def solution(mesh):
    n_row, n_proto = mesh.shape["row"], mesh.shape["proto"]
    side = math.isqrt(n_row)
    n_z = n_proto // 2
    far = max(n_z // 2, 1)

    def shards(embeddings, prototypes, block_mask):
        rows, depth = embeddings.shape
        protos, slab = prototypes.shape
        share = depth // n_proto
        row_tiles, col_tiles = rows // TILE, protos // TILE
        log_column = math.log2((rows * n_row) / (protos * n_proto))
        f32, bf16 = jnp.float32, jnp.bfloat16
        dma = pltpu.SemaphoreType.DMA
        peers_r, peers_p = max(n_row - 1, 1), max(n_proto - 1, 1)
        vmem = pl.BlockSpec(memory_space=pltpu.VMEM)
        targets, row_potential, column_potential = pl.pallas_call(
            functools.partial(kernel, (side, n_row, n_proto, log_column)),
            out_shape=(
                jax.ShapeDtypeStruct((share, rows), bf16),
                jax.ShapeDtypeStruct((row_tiles, TILE), f32),
                jax.ShapeDtypeStruct((col_tiles, TILE), f32),
            ),
            in_specs=[
                vmem,
                pl.BlockSpec(memory_space=pl.ANY),
                pl.BlockSpec(memory_space=pltpu.SMEM),
            ],
            out_specs=(vmem, vmem, vmem),
            scratch_shapes=[
                pltpu.VMEM((rows, depth), bf16),
                pltpu.VMEM((depth, protos), bf16),
                pltpu.VMEM((rows, protos), f32),
                pltpu.VMEM((rows, TILE), f32),
                pltpu.VMEM((ITERS, row_tiles, TILE), f32),
                pltpu.VMEM((ITERS, peers_p, row_tiles, TILE), f32),
                pltpu.VMEM((ITERS, col_tiles, TILE), f32),
                pltpu.VMEM((ITERS, peers_r, col_tiles, TILE), f32),
                pltpu.VMEM((n_z, 2 * share, rows), bf16),
                pltpu.VMEM((n_z, share, rows), bf16),
                pltpu.VMEM((2, far, 2, share, rows // 2), bf16),
                pltpu.VMEM((2, far, 2, share, rows // 2), bf16),
                dma(()),
                dma((2, 20)),
                dma((2, 20)),
                dma((ITERS,)),
                dma((ITERS,)),
                dma((ITERS,)),
                dma((ITERS,)),
                dma((n_z,)),
                dma((n_z,)),
                dma((2, far, 2)),
                dma((2, far, 2)),
            ],
            compiler_params=pltpu.CompilerParams(
                collective_id=0, has_side_effects=True, vmem_limit_bytes=56 * 1024 * 1024
            ),
        )(prototypes.T, embeddings, block_mask)
        return (
            targets.T,
            row_potential.reshape(rows),
            column_potential.reshape(protos),
        )

    return jax.shard_map(
        shards,
        mesh=mesh,
        in_specs=(P("row", None), P("proto", "row"), P("row", "proto")),
        out_specs=(P("row", "proto"), P("row"), P("proto")),
        check_vma=False,
    )
```

time: 576 us -> 124 us (0.22)
  blocking collectives: 353 us -> 0 us
  waiting for transfers between devices: 125 us -> 0 us
  Pallas kernels: 0 us -> 117 us
  other arithmetic: 51.8 us -> 0 us
  matrix products: 22.2 us -> 0 us
  between operations: 14.2 us -> 0.64 us
    pmax x6 -> x0, blocking collectives: 193 us -> none  [the longest x3 102 us: row_logsum(): lax.pmax(jnp.max(jnp.where(allowed, values, NEGATIVE), axis=1), 'proto')]
    psum x6 -> x0, blocking collectives: 159 us -> none  [the longest x3 85.7 us: column_logsum(): lax.psum(jnp.sum(jnp.where(allowed, jnp.exp(values - peak[None, :]), 0.0)...]
    pallas_call x0 -> x1, Pallas kernels: none -> 117 us  [shards(): pl.pallas_call(functools.partial(kernel, (side, n_row, n_proto, log_colum...]
    reduce_scatter x1 -> x0, waiting for transfers between devices: 69.9 us -> none  [shards(): lax.psum_scatter(partial_value.astype(jnp.bfloat16), 'proto', scatter_dim...]
    all_gather x1 -> x0, waiting for transfers between devices: 54.6 us -> none  [shards(): features = lax.all_gather(prototypes, 'row', axis=1, tiled=True)]
    reduce_sum x6 -> x0, other arithmetic: 28.3 us -> none  [the longest x3 14.3 us: row_logsum(): jnp.sum(jnp.where(allowed, jnp.exp(values - peak[:, None]), 0.0), axis=1)]
    reduce_max x5 -> x0, other arithmetic: 22.8 us -> none  [the longest x3 12.8 us: column_logsum(): jnp.max(jnp.where(allowed, values, NEGATIVE), axis=0)]
    dot_general x2 -> x0, matrix products: 22.2 us -> none  [the longest x1 11.4 us: shards(): lax.dot_general(embeddings, features, (((1,), (1,)), ((), ())), preferred...]
  transfers between devices with their start and end apart: 2 -> 0, of which waited for: 2 -> 0; matrix products, arithmetic and copies ran while one was open for 0% -> 0% of each run, Pallas kernels for 0% -> 0%
where the time goes in v1:
time: 124 us; the launch traced here: 123 us
  Pallas kernels  117 us (94%)
  local copies, waits for them, and re-layouts  5.6 us (5%)
    pallas_call x1, Pallas kernels, shards(): pl.pallas_call(functools.partial(kernel, (side, n_row, n_proto, log_colum...  117 us
    unnamed x4, local copies, waits for them, and re-layouts  5.6 us

profile of v1, /device:TPU:1, one launch (start us, length us, event | category | flops | bytes accessed | tf_op | source)
XLA Modules:
  0.0 123.4 jit_solution(9562771786945908032)
XLA Ops:
  0.6 1.4 %copy.6.mask_ref = s32[16,8]{1,0:T(8,128)} copy(s32[16,8]{0,1:T(8,128)} %param.5) | data formatting | bytes 1024 | tf_op args[2]
  2.0 117.2 %shard_map.58 = (bf16[64,2048]{1,0:T(8,128)(2,1)}, f32[16,128]{1,0:T(8,128)}, f32[8,128]{1,0:T(8,128)}) custom-call(bf16[64,1024]{1,0:T(8,128)(2,1)} %bitcast.5, bf16[2048,1024]{1,0:T(8,128)(2,1)} %emb_hbm.1, s32[16,8]{1,0:T(8,128)} %copy.6.mask_ref), custom_call_target="tpu_custom_call" | custom-call | tf_op jit(solution)/shard_map/pallas_call | solution.py:433
  119.2 1.7 %copy.10 = bf16[2048,64]{0,1:T(8,128)(2,1)} copy(bf16[2048,64]{0,1:T(8,128)(2,1)} %bitcast.4) | data formatting | bytes 524288
  120.9 1.3 %copy.11 = f32[2048]{0:T(1024)} copy(f32[2048]{0:T(1024)} %bitcast.6) | data formatting | bytes 16384
  122.2 1.3 %copy.12 = f32[1024]{0:T(1024)} copy(f32[1024]{0:T(1024)} %bitcast.7) | data formatting | bytes 8192

commit v2 on v1

--- a/solution.py
+++ b/solution.py
@@ -14,6 +14,7 @@
 LOWEST = -1e38
 LOG2E = 1.4426950408889634
 LN2 = 0.6931471805599453
+SPLIT = 4
 MESH = pl.DeviceIdType.MESH
 
 
@@ -34,6 +35,7 @@
     col_out,
     emb,
     feat,
+    feat_t,
     sim,
     wide,
     row_send,
@@ -182,44 +184,47 @@
 
     emb_copy.wait()
 
-    mm, mn = min(512, rows), min(256, protos)
-
-    def score_block(step, carry):
-        i, j = step // (protos // mn), lax.rem(step, protos // mn)
+    mm = min(512, rows)
+
+    def lane_lse(vals):
+        peak = tree_reduce(jnp.maximum, vals)
+        return peak + jnp.log2(tree_reduce(jnp.add, [jnp.exp2(v - peak) for v in vals]))
+
+    def score_block(i, carry):
         row0 = pl.multiple_of(i * mm, mm)
-        col0 = pl.multiple_of(j * mn, mn)
-        acc = jnp.dot(
-            emb[pl.ds(row0, mm), :], feat[:, pl.ds(col0, mn)], preferred_element_type=jnp.float32
-        )
+        acc = jnp.dot(emb[pl.ds(row0, mm), :], feat[...], preferred_element_type=jnp.float32)
         for a in range(mm // TILE):
-            for b in range(mn // TILE):
-                allowed = mask_ref[i * (mm // TILE) + a, j * (mn // TILE) + b] == 1
-                bias = jnp.where(allowed, 0.0, NEGATIVE)
-                sim[
-                    pl.ds(pl.multiple_of(row0 + a * TILE, TILE), TILE),
-                    pl.ds(pl.multiple_of(col0 + b * TILE, TILE), TILE),
-                ] = acc[a * TILE : (a + 1) * TILE, b * TILE : (b + 1) * TILE] * scale + bias
+            bias = [
+                jnp.where(mask_ref[j, i * (mm // TILE) + a] == 1, 0.0, NEGATIVE)
+                for j in range(col_tiles)
+            ]
+            for g in range(a * TILE, (a + 1) * TILE, 8):
+                vals = [
+                    acc[g : g + 8, j * TILE : (j + 1) * TILE] * scale + bias[j]
+                    for j in range(col_tiles)
+                ]
+                for j in range(col_tiles):
+                    sim[pl.ds(row0 + g, 8), j * TILE : (j + 1) * TILE] = vals[j]
+                wide[pl.ds(row0 + g, 8), :] = lane_lse(vals)
         return carry
 
-    lax.fori_loop(0, (rows // mm) * (protos // mn), score_block, 0)
-
-    group = 16
+    lax.fori_loop(0, rows // mm, score_block, 0)
+
+    group = 64
+
+    def lanes(shifts):
+        return [jnp.broadcast_to(shifts[j : j + 1, :], (8, TILE)) for j in range(col_tiles)]
 
     def row_partial(shifts):
         def block(step, carry):
             base = pl.multiple_of(step * group, group)
-            vals = []
-            for j in range(col_tiles):
-                v = sim[pl.ds(base, group), j * TILE : (j + 1) * TILE]
-                if shifts is not None:
-                    v = v + shifts[j : j + 1, :]
-                vals.append(v)
-            peak = tree_reduce(jnp.maximum, vals)
-            total = tree_reduce(jnp.add, [jnp.exp2(v - peak) for v in vals])
-            wide[pl.ds(base, group), :] = peak + jnp.log2(total)
+            for g in range(0, group, 8):
+                wide[pl.ds(base + g, 8), :] = lane_lse(
+                    [sim[pl.ds(base + g, 8), j * TILE : (j + 1) * TILE] + shifts[j] for j in range(col_tiles)]
+                )
             return carry
 
-        lax.fori_loop(0, rows // group, block, 0, unroll=2)
+        lax.fori_loop(0, rows // group, block, 0)
 
     def row_finish(k):
         def block(i, carry):
@@ -231,8 +236,8 @@
 
         lax.fori_loop(0, row_tiles, block, 0, unroll=4)
 
-    def exchange(send, recv, send_sem, recv_sem, k, n, target):
-        for d in range(1, n):
+    def exchange_start(send, recv, send_sem, recv_sem, k, n, target, near):
+        for d in sorted(range(1, n), key=lambda d: (-near(d), d)):
             pltpu.make_async_remote_copy(
                 src_ref=send.at[k],
                 dst_ref=recv.at[k, d - 1],
@@ -241,6 +246,8 @@
                 device_id=target(d),
                 device_id_type=MESH,
             ).start()
+
+    def exchange_end(send, recv, send_sem, recv_sem, k, n, target):
         if n > 1:
             pltpu.make_async_remote_copy(
                 src_ref=recv.at[k],
@@ -287,67 +294,101 @@
             total = jnp.sum(jnp.exp2(level - peak), axis=0, keepdims=True)
             col_send[k, j : j + 1, :] = peak + jnp.log2(total)
 
+    def proto_peer(d):
+        return (r, lax.rem(p + d, n_proto))
+
+    def row_peer(d):
+        return (lax.rem(r + d, n_row), p)
+
+    def wrap(d, n):
+        return min(d, n - d)
+
     shifts = None
     for k in range(ITERS):
-        row_partial(shifts)
+        if k > 0:
+            row_partial(lanes(shifts))
         row_finish(k)
-        row_out[...] = -exchange(
-            row_send, row_recv, rs_sem, rr_sem, k, n_proto, lambda d: (r, lax.rem(p + d, n_proto))
-        )
+        exchange_start(
+            row_send, row_recv, rs_sem, rr_sem, k, n_proto, proto_peer, lambda d: wrap(d, n_proto)
+        )
+        if k == 0:
+            for i in range(0, protos, TILE):
+                for j in range(0, depth, TILE):
+                    feat_t[i : i + TILE, j : j + TILE] = jnp.transpose(feat[j : j + TILE, i : i + TILE])
+        row_out[...] = -exchange_end(row_send, row_recv, rs_sem, rr_sem, k, n_proto, proto_peer)
         spread_rows()
         column_partial(k)
-        shifts = log_column - exchange(
-            col_send, col_recv, cs_sem, cr_sem, k, n_row, lambda d: (lax.rem(r + d, n_row), p)
-        )
+        exchange_start(
+            col_send,
+            col_recv,
+            cs_sem,
+            cr_sem,
+            k,
+            n_row,
+            row_peer,
+            lambda d: wrap(d // side, side) + wrap(d % side, side),
+        )
+        shifts = log_column - exchange_end(col_send, col_recv, cs_sem, cr_sem, k, n_row, row_peer)
 
     col_out[...] = shifts * LN2
+    shifts = lanes(shifts)
 
     plan = emb
-
-    def plan_block(step, carry):
-        base = pl.multiple_of(step * group, group)
-        u = wide[pl.ds(base, group), :]
-        for j in range(col_tiles):
-            v = sim[pl.ds(base, group), j * TILE : (j + 1) * TILE] + (u + shifts[j : j + 1, :])
-            plan[pl.ds(base, group), j * TILE : (j + 1) * TILE] = jnp.exp2(v).astype(jnp.bfloat16)
-        return carry
-
-    lax.fori_loop(0, rows // group, plan_block, 0, unroll=2)
-    row_out[...] = row_out[...] * LN2
-
-    width = rows // 2
-    tn = min(256, rows)
-
-    def product(t):
-        feat0 = pl.multiple_of(lax.rem(z + t, n_z) * 2 * share, 2 * share)
-
-        def block(n, carry):
-            row0 = pl.multiple_of(n * tn, tn)
-            part[t, :, pl.ds(row0, tn)] = lax.dot_general(
-                feat[pl.ds(feat0, 2 * share), :],
-                plan[pl.ds(row0, tn), :],
-                (((1,), (1,)), ((), ())),
-                preferred_element_type=jnp.float32,
-            ).astype(jnp.bfloat16)
-            return carry
-
-        lax.fori_loop(0, rows // tn, block, 0)
-
-    def sibling_copy(t):
+    far = n_z // 2
+    order = [far] + [t for d in range(far - 1, 0, -1) for t in (d, n_z - d)] + [0] if far else [0]
+    pairs = [order[i : i + 2] for i in range(0, len(order), 2)]
+    width = rows // SPLIT
+    mp = rows // 2
+    sent_sibling = []
+
+    def plan_block(base):
+        for g in range(0, mp, 16):
+            shift = [wide[pl.ds(base + g + e, 8), :] for e in (0, 8)]
+            for j in range(col_tiles):
+                v = [
+                    jnp.exp2(sim[pl.ds(base + g + e, 8), j * TILE : (j + 1) * TILE] + (shift[e // 8] + shifts[j]))
+                    for e in (0, 8)
+                ]
+                plan[pl.ds(base + g, 16), j * TILE : (j + 1) * TILE] = jnp.concatenate(v, axis=0).astype(
+                    jnp.bfloat16
+                )
+
+    def product(ts, base):
+        weights = [
+            feat_t[:, pl.ds(pl.multiple_of(lax.rem(z + t, n_z) * 2 * share, 2 * share), 2 * share)] for t in ts
+        ]
+        acc = jnp.dot(
+            plan[pl.ds(base, mp), :],
+            jnp.concatenate(weights, axis=1) if len(ts) > 1 else weights[0],
+            preferred_element_type=jnp.float32,
+        )
+        for i, t in enumerate(ts):
+            part[t, :, pl.ds(base, mp)] = jnp.transpose(acc[:, i * 2 * share : (i + 1) * 2 * share]).astype(
+                jnp.bfloat16
+            )
+
+    def sibling_copy(t, h):
         other = 1 - c
         return pltpu.make_async_remote_copy(
-            src_ref=part.at[t, pl.ds(pl.multiple_of(other * share, share), share), :],
-            dst_ref=sib_recv.at[t],
-            send_sem=ss_sem.at[t],
-            recv_sem=sr_sem.at[t],
+            src_ref=part.at[t, pl.ds(pl.multiple_of(other * share, share), share), h * width : (h + 1) * width],
+            dst_ref=sib_recv.at[t, h],
+            send_sem=ss_sem.at[t, h],
+            recv_sem=sr_sem.at[t, h],
             device_id=(r, z * 2 + other),
             device_id_type=MESH,
         )
 
+    def to_sibling(ts, hs):
+        for t in ts:
+            for h in hs:
+                copy = sibling_copy(t, h)
+                copy.start()
+                sent_sibling.append(copy)
+
     def chip_sum(t, h):
+        sibling_copy(t, h).wait_recv()
         mine = part[t, pl.ds(pl.multiple_of(c * share, share), share), h * width : (h + 1) * width]
-        theirs = sib_recv[t, :, h * width : (h + 1) * width]
-        return mine.astype(jnp.float32) + theirs.astype(jnp.float32)
+        return mine.astype(jnp.float32) + sib_recv[t, h].astype(jnp.float32)
 
     def chain_copy(way, d, h):
         step = 1 if way == 0 else n_z - 1
@@ -360,58 +401,76 @@
             device_id_type=MESH,
         )
 
-    far = n_z // 2
     flying = []
-
-    def forward(way, d, h):
+    lower, upper = list(range(SPLIT // 2)), list(range(SPLIT // 2, SPLIT))
+    whole_way = (lower, upper)
+    rest = (upper, lower)
+
+    def forward(way, d, hs):
         t = d if way == 0 else n_z - d
-        value = chip_sum(t, h)
-        if d < far and (d + 1 < far or h == way):
-            chain_copy(way, d + 1, h).wait_recv()
-            value = value + rx[way, d, h].astype(jnp.float32)
-        tx[way, d - 1, h] = value.astype(jnp.bfloat16)
-        copy = chain_copy(way, d, h)
-        copy.start()
-        flying.append(copy)
-
-    def ready(t):
-        product(t)
-        copy = sibling_copy(t)
-        copy.start()
-        return copy
-
-    waiting = {}
-    order = [far] + [t for d in range(far - 1, 0, -1) for t in (d, n_z - d)] + [0] if far else [0]
-    for t in order[:3]:
-        waiting[t] = ready(t)
+        for h in hs:
+            value = chip_sum(t, h)
+            if d < far and (d + 1 < far or h in whole_way[way]):
+                chain_copy(way, d + 1, h).wait_recv()
+                value = value + rx[way, d, h].astype(jnp.float32)
+            tx[way, d - 1, h] = value.astype(jnp.bfloat16)
+            copy = chain_copy(way, d, h)
+            copy.start()
+            flying.append(copy)
+
+    def later_pair(n):
+        if n < len(pairs):
+
+            def block(i, carry):
+                product(pairs[n], pl.multiple_of(i * mp, mp))
+                return carry
+
+            lax.fori_loop(0, 2, block, 0)
+            to_sibling(pairs[n], lower + upper)
+
+    for i, hs in enumerate((lower, upper)):
+        plan_block(i * mp)
+        product(pairs[0], i * mp)
+        to_sibling(pairs[0], hs)
     if far:
-        waiting[far].wait()
-        forward(0, far, 0)
-        forward(1, far, 1)
-    done = 3
-    for d in range(far - 1, 0, -1):
-        for t in (d, n_z - d):
-            waiting[t].wait()
-        forward(0, d, 1)
-        forward(1, d, 0)
-        for t in order[done : done + 2]:
-            waiting[t] = ready(t)
-        done += 2
-        forward(0, d, 0)
-        forward(1, d, 1)
-    for t in order[done:]:
-        waiting[t] = ready(t)
-    waiting[0].wait()
-    for h in (1, 0):
+        forward(0, far, lower)
+        forward(1, far, upper)
+    if far > 1:
+        forward(0, far - 1, upper)
+    later_pair(1)
+    if far > 1:
+        forward(1, far - 1, lower)
+    later_pair(2)
+    if far > 1:
+        forward(0, far - 1, lower)
+        forward(1, far - 1, upper)
+    later_pair(3)
+    for d in range(far - 2, 0, -1):
+        for h, g in zip(upper + lower, lower + upper):
+            forward(0, d, [h])
+            forward(1, d, [g])
+    for h in upper + lower:
         value = chip_sum(0, h)
         for way in (0, 1):
-            if far > 1 or (far == 1 and h == way):
+            if far > 1 or (far == 1 and h in whole_way[way]):
                 chain_copy(way, 1, h).wait_recv()
                 value = value + rx[way, 0, h].astype(jnp.float32)
         out_ref[:, h * width : (h + 1) * width] = value.astype(jnp.bfloat16)
-
-    for copy in sent + flying:
+    row_out[...] = row_out[...] * LN2
+
+    for copy in sent + sent_sibling + flying:
         copy.wait_send()
+
+
+def hand_over(a, b, c, a_out, b_out, c_out, sem):
+    copies = [
+        pltpu.make_async_copy(src, dst, sem.at[i])
+        for i, (src, dst) in enumerate(((a, a_out), (b, b_out), (c, c_out)))
+    ]
+    for copy in copies:
+        copy.start()
+    for copy in copies:
+        copy.wait()
 
 
 def solution(mesh):
@@ -430,13 +489,14 @@
         dma = pltpu.SemaphoreType.DMA
         peers_r, peers_p = max(n_row - 1, 1), max(n_proto - 1, 1)
         vmem = pl.BlockSpec(memory_space=pltpu.VMEM)
-        targets, row_potential, column_potential = pl.pallas_call(
+        shapes = (
+            jax.ShapeDtypeStruct((share, rows), bf16),
+            jax.ShapeDtypeStruct((row_tiles, TILE), f32),
+            jax.ShapeDtypeStruct((col_tiles, TILE), f32),
+        )
+        results = pl.pallas_call(
             functools.partial(kernel, (side, n_row, n_proto, log_column)),
-            out_shape=(
-                jax.ShapeDtypeStruct((share, rows), bf16),
-                jax.ShapeDtypeStruct((row_tiles, TILE), f32),
-                jax.ShapeDtypeStruct((col_tiles, TILE), f32),
-            ),
+            out_shape=shapes,
             in_specs=[
                 vmem,
                 pl.BlockSpec(memory_space=pl.ANY),
@@ -446,6 +506,7 @@
             scratch_shapes=[
                 pltpu.VMEM((rows, depth), bf16),
                 pltpu.VMEM((depth, protos), bf16),
+                pltpu.VMEM((protos, depth), bf16),
                 pltpu.VMEM((rows, protos), f32),
                 pltpu.VMEM((rows, TILE), f32),
                 pltpu.VMEM((ITERS, row_tiles, TILE), f32),
@@ -453,9 +514,9 @@
                 pltpu.VMEM((ITERS, col_tiles, TILE), f32),
                 pltpu.VMEM((ITERS, peers_r, col_tiles, TILE), f32),
                 pltpu.VMEM((n_z, 2 * share, rows), bf16),
-                pltpu.VMEM((n_z, share, rows), bf16),
-                pltpu.VMEM((2, far, 2, share, rows // 2), bf16),
-                pltpu.VMEM((2, far, 2, share, rows // 2), bf16),
+                pltpu.VMEM((n_z, SPLIT, share, rows // SPLIT), bf16),
+                pltpu.VMEM((2, far, SPLIT, share, rows // SPLIT), bf16),
+                pltpu.VMEM((2, far, SPLIT, share, rows // SPLIT), bf16),
                 dma(()),
                 dma((2, 20)),
                 dma((2, 20)),
@@ -463,15 +524,23 @@
                 dma((ITERS,)),
                 dma((ITERS,)),
                 dma((ITERS,)),
-                dma((n_z,)),
-                dma((n_z,)),
-                dma((2, far, 2)),
-                dma((2, far, 2)),
+                dma((n_z, SPLIT)),
+                dma((n_z, SPLIT)),
+                dma((2, far, SPLIT)),
+                dma((2, far, SPLIT)),
             ],
             compiler_params=pltpu.CompilerParams(
                 collective_id=0, has_side_effects=True, vmem_limit_bytes=56 * 1024 * 1024
             ),
-        )(prototypes.T, embeddings, block_mask)
+        )(prototypes.T, embeddings, block_mask.T)
+        anywhere = pl.BlockSpec(memory_space=pl.ANY)
+        targets, row_potential, column_potential = pl.pallas_call(
+            hand_over,
+            out_shape=shapes,
+            in_specs=[anywhere] * 3,
+            out_specs=(anywhere,) * 3,
+            scratch_shapes=[dma((3,))],
+        )(*results)
         return (
             targets.T,
             row_potential.reshape(rows),

time: 124 us -> 113 us (0.911)
  local copies, waits for them, and re-layouts: 5.6 us -> 0 us
  Pallas kernels: 117 us -> 113 us
    pallas_call x1, Pallas kernels: 117 us -> 103 us  [shards(): pl.pallas_call(functools.partial(kernel, (side, n_row, n_proto, log_colum...]
    pallas_call x0 -> x1, Pallas kernels: none -> 9.44 us  [shards(): pl.pallas_call(hand_over, out_shape=shapes, in_specs=[anywhere] * 3, out_...]
    unnamed x4 -> x0, local copies, waits for them, and re-layouts: 5.6 us -> none
where the time goes in v2:
time: 113 us
  Pallas kernels  113 us (100%)
    pallas_call x1, Pallas kernels, shards(): pl.pallas_call(functools.partial(kernel, (side, n_row, n_proto, log_colum...  103 us
    pallas_call x1, Pallas kernels, shards(): pl.pallas_call(hand_over, out_shape=shapes, in_specs=[anywhere] * 3, out_...  9.44 us

profile of v2, /device:TPU:1, one launch (start us, length us, event | category | flops | bytes accessed | tf_op | source)
XLA Modules:
  0.0 113.3 jit_solution(10579407520417999603)
XLA Ops:
  0.6 103.2 %shard_map.58 = (bf16[64,2048]{1,0:T(8,128)(2,1)}, f32[16,128]{1,0:T(8,128)}, f32[8,128]{1,0:T(8,128)}) custom-call(bf16[64,1024]{1,0:T(8,128)(2,1)} %bitcast.5, bf16[2048,1024]{1,0:T(8,128)(2,1)} %emb_hbm.1, s32[8,16]{1,0:T(8,128)} %bitcast.6), custom_call_target="tpu_custom_call" | custom-call | tf_op jit(solution)/shard_map/pallas_call | solution.py:497
  103.9 9.4 %shard_map.59 = (bf16[64,2048]{1,0:T(8,128)(2,1)}, f32[16,128]{1,0:T(8,128)}, f32[8,128]{1,0:T(8,128)}) custom-call(bf16[64,2048]{1,0:T(8,128)(2,1)} %get-tuple-element.9.a, f32[16,128]{1,0:T(8,128)} %get-tuple-element.10.b, f32[8,128]{1,0:T(8,128)} %get-tuple-element.11.c), custom_call_target="tpu_custom_call" | custom-call | tf_op jit(solution)/shard_map/pallas_call | solution.py:537

commit v3 on v2

--- a/solution.py
+++ b/solution.py
@@ -15,6 +15,7 @@
 LOG2E = 1.4426950408889634
 LN2 = 0.6931471805599453
 SPLIT = 4
+PARTS = 2
 MESH = pl.DeviceIdType.MESH
 
 
@@ -90,132 +91,162 @@
     pl.semaphore_wait(barrier, n_row + n_proto - 2)
 
     half, quarter = slab // 2, slab // 4
+    span = protos // PARTS
 
     def shift(tree, df, ds):
         return (ds, df) if tree == 0 else (df, ds)
 
-    def piece(tree, df, ds, which, ref=None):
+    def piece(n, tree, df, ds, which, ref=None):
         start = tree * half + (quarter if which == "hi" else 0)
         size = half if which == "all" else quarter
-        if ref is not None:
-            return ref.at[pl.ds(start, size), :]
-        return feat.at[pl.ds(pl.multiple_of(row_of(*shift(tree, df, ds)) * slab + start, quarter), size), :]
-
-    moves = {}
-
-    def gather_copy(tree, key, src_at, move, which, from_own):
-        slot = moves.setdefault((tree, key), len([k for k in moves if k[0] == tree]))
-        block = piece(tree, *src_at, which)
-        src = piece(tree, 0, 0, which, own_ref) if from_own else block
+        if ref is None:
+            ref = feat
+            start = pl.multiple_of(row_of(*shift(tree, df, ds)) * slab + start, quarter)
+        return ref.at[pl.ds(start, size), n * span : (n + 1) * span]
+
+    slots = {}
+    for sign in "+-":
+        for key in ("f", "g", "s0", "s-1", "s1", "s2", "t0", "t-1", "t1", "t2"):
+            slots[key + sign] = len(slots)
+    towards = {"+": 1, "-": -1}
+
+    def gather_copy(n, tree, key, at, which, from_own=False):
+        way = towards[key[-1]]
+        move = (way, 0) if key[0] in "fg" else (0, way)
+        block = piece(n, tree, *at, which)
         return pltpu.make_async_remote_copy(
-            src_ref=src,
+            src_ref=piece(n, tree, 0, 0, which, own_ref) if from_own else block,
             dst_ref=block,
-            send_sem=gs_sem.at[tree, slot],
-            recv_sem=gr_sem.at[tree, slot],
+            send_sem=gs_sem.at[n, tree, slots[key]],
+            recv_sem=gr_sem.at[n, tree, slots[key]],
             device_id=(row_of(*shift(tree, *move)), p),
             device_id_type=MESH,
         )
 
     sent = []
 
-    def push(tree, key, src_at, move, which, from_own=False):
-        copy = gather_copy(tree, key, src_at, move, which, from_own)
+    def push(n, tree, key, at, which, from_own=False):
+        copy = gather_copy(n, tree, key, at, which, from_own)
         copy.start()
         sent.append(copy)
 
-    if n_row > 1:
+    def arrive(n, tree, key, at, which):
+        gather_copy(n, tree, key, at, which).wait_recv()
+
+    def across(n, t, df):
+        push(n, t, "s%d+" % df, (df, 0), "all")
+        push(n, t, "s%d-" % df, (df, 0), "all")
+
+    def relay(n, t, df):
+        arrive(n, t, "s%d+" % df, (df, -1), "all")
+        push(n, t, "t%d+" % df, (df, -1), "lo")
+        arrive(n, t, "s%d-" % df, (df, 1), "all")
+        push(n, t, "t%d-" % df, (df, 1), "hi")
+
+    def gather_stage(stage, n):
+        if n_row == 1:
+            return
         trees = (0, 1)
-        for t in trees:
-            push(t, "f+", (0, 0), (1, 0), "all", True)
-            push(t, "f-", (0, 0), (-1, 0), "all", True)
-        for t in trees:
-            push(t, "s+0", (0, 0), (0, 1), "all", True)
-            push(t, "s-0", (0, 0), (0, -1), "all", True)
-
+        if stage == 0:
+            for t in trees:
+                push(n, t, "f+", (0, 0), "all", True)
+                push(n, t, "f-", (0, 0), "all", True)
+            for t in trees:
+                push(n, t, "s0+", (0, 0), "all", True)
+                push(n, t, "s0-", (0, 0), "all", True)
+        elif stage == 1:
+            for t in trees:
+                arrive(n, t, "f+", (-1, 0), "all")
+                push(n, t, "g+", (-1, 0), "lo")
+                arrive(n, t, "f-", (1, 0), "all")
+                push(n, t, "g-", (1, 0), "hi")
+            for t in trees:
+                across(n, t, -1)
+                across(n, t, 1)
+        elif stage == 2:
+            for t in trees:
+                relay(n, t, 0)
+        elif stage == 3:
+            for t in trees:
+                arrive(n, t, "g+", (2, 0), "lo")
+                arrive(n, t, "g-", (2, 0), "hi")
+                across(n, t, 2)
+        elif stage == 4:
+            for t in trees:
+                relay(n, t, -1)
+                relay(n, t, 1)
+        elif stage == 5:
+            for t in trees:
+                relay(n, t, 2)
+        elif stage == 6:
+            for t in trees:
+                for df in (0, -1, 1, 2):
+                    arrive(n, t, "t%d+" % df, (df, 2), "lo")
+                    arrive(n, t, "t%d-" % df, (df, 2), "hi")
+
+    for n in range(PARTS):
+        gather_stage(0, n)
     feat[pl.ds(pl.multiple_of(r * slab, slab), slab), :] = own_ref[...]
-
-    if n_row > 1:
-
-        def across(t, df):
-            push(t, "s+%d" % df, (df, 0), (0, 1), "all")
-            push(t, "s-%d" % df, (df, 0), (0, -1), "all")
-
-        def relay(t, df):
-            arrive(t, "s+%d" % df, (df, -1), (0, 1))
-            push(t, "t+%d" % df, (df, -1), (0, 1), "lo")
-            arrive(t, "s-%d" % df, (df, 1), (0, -1))
-            push(t, "t-%d" % df, (df, 1), (0, -1), "hi")
-
-        def arrive(t, key, at, move, which="all"):
-            slot = moves[(t, key)]
-            block = piece(t, *at, which)
-            pltpu.make_async_remote_copy(
-                src_ref=block,
-                dst_ref=block,
-                send_sem=gs_sem.at[t, slot],
-                recv_sem=gr_sem.at[t, slot],
-                device_id=(row_of(*shift(t, *move)), p),
-                device_id_type=MESH,
-            ).wait_recv()
-
-        for t in trees:
-            arrive(t, "f+", (-1, 0), (1, 0))
-            push(t, "g+", (-1, 0), (1, 0), "lo")
-            arrive(t, "f-", (1, 0), (-1, 0))
-            push(t, "g-", (1, 0), (-1, 0), "hi")
-        for t in trees:
-            across(t, -1)
-            across(t, 1)
-        for t in trees:
-            relay(t, 0)
-        for t in trees:
-            arrive(t, "g+", (2, 0), (1, 0), "lo")
-            arrive(t, "g-", (2, 0), (-1, 0), "hi")
-            across(t, 2)
-        for t in trees:
-            relay(t, -1)
-            relay(t, 1)
-        for t in trees:
-            relay(t, 2)
-        for t in trees:
-            for df in (0, -1, 1, 2):
-                arrive(t, "t+%d" % df, (df, 2), (0, 1), "lo")
-                arrive(t, "t-%d" % df, (df, 2), (0, -1), "hi")
+    for stage in (1, 2, 3, 4):
+        for n in range(PARTS):
+            gather_stage(stage, n)
+    gather_stage(5, 0)
+    gather_stage(6, 0)
 
     emb_copy.wait()
 
-    mm = min(512, rows)
+    mm = min(512, rows // 2)
 
     def lane_lse(vals):
         peak = tree_reduce(jnp.maximum, vals)
         return peak + jnp.log2(tree_reduce(jnp.add, [jnp.exp2(v - peak) for v in vals]))
 
-    def score_block(i, carry):
-        row0 = pl.multiple_of(i * mm, mm)
-        acc = jnp.dot(emb[pl.ds(row0, mm), :], feat[...], preferred_element_type=jnp.float32)
-        for a in range(mm // TILE):
-            bias = [
-                jnp.where(mask_ref[j, i * (mm // TILE) + a] == 1, 0.0, NEGATIVE)
-                for j in range(col_tiles)
-            ]
-            for g in range(a * TILE, (a + 1) * TILE, 8):
-                vals = [
-                    acc[g : g + 8, j * TILE : (j + 1) * TILE] * scale + bias[j]
-                    for j in range(col_tiles)
+    span_tiles = span // TILE
+
+    def score_blocks(n, first, last):
+        def block(i, carry):
+            row0 = pl.multiple_of(i * mm, mm)
+            acc = jnp.dot(
+                emb[pl.ds(row0, mm), :],
+                feat[:, n * span : (n + 1) * span],
+                preferred_element_type=jnp.float32,
+            )
+            for a in range(mm // TILE):
+                bias = [
+                    jnp.where(mask_ref[n * span_tiles + j, i * (mm // TILE) + a] == 1, 0.0, NEGATIVE)
+                    for j in range(span_tiles)
                 ]
-                for j in range(col_tiles):
-                    sim[pl.ds(row0 + g, 8), j * TILE : (j + 1) * TILE] = vals[j]
-                wide[pl.ds(row0 + g, 8), :] = lane_lse(vals)
-        return carry
-
-    lax.fori_loop(0, rows // mm, score_block, 0)
+                for g in range(a * TILE, (a + 1) * TILE, 8):
+                    vals = [
+                        acc[g : g + 8, j * TILE : (j + 1) * TILE] * scale + bias[j]
+                        for j in range(span_tiles)
+                    ]
+                    for j in range(span_tiles):
+                        col0 = (n * span_tiles + j) * TILE
+                        sim[pl.ds(row0 + g, 8), col0 : col0 + TILE] = vals[j]
+                    if n > 0:
+                        vals.append(wide[pl.ds(row0 + g, 8), :])
+                    wide[pl.ds(row0 + g, 8), :] = lane_lse(vals)
+            return carry
+
+        lax.fori_loop(first, last, block, 0)
+
+    blocks = rows // mm
+    score_blocks(0, 0, max(blocks // 4, 1))
+    for n in range(1, PARTS):
+        gather_stage(5, n)
+    score_blocks(0, max(blocks // 4, 1), blocks)
+    for n in range(1, PARTS):
+        gather_stage(6, n)
 
     group = 64
 
     def lanes(shifts):
         return [jnp.broadcast_to(shifts[j : j + 1, :], (8, TILE)) for j in range(col_tiles)]
 
-    def row_partial(shifts):
+    half_rows, half_tiles = rows // 2, row_tiles // 2
+
+    def row_partial(shifts, part):
         def block(step, carry):
             base = pl.multiple_of(step * group, group)
             for g in range(0, group, 8):
@@ -224,53 +255,53 @@
                 )
             return carry
 
-        lax.fori_loop(0, rows // group, block, 0)
-
-    def row_finish(k):
+        lax.fori_loop(part * half_rows // group, (part + 1) * half_rows // group, block, 0)
+
+    def row_finish(k, part):
         def block(i, carry):
             t = jnp.transpose(wide[pl.ds(pl.multiple_of(i * TILE, TILE), TILE), :])
             peak = jnp.max(t, axis=0, keepdims=True)
             total = jnp.sum(jnp.exp2(t - peak), axis=0, keepdims=True)
-            row_send[k, pl.ds(i, 1), :] = peak + jnp.log2(total)
+            row_send[k, part, pl.ds(i - part * half_tiles, 1), :] = peak + jnp.log2(total)
             return carry
 
-        lax.fori_loop(0, row_tiles, block, 0, unroll=4)
-
-    def exchange_start(send, recv, send_sem, recv_sem, k, n, target, near):
+        lax.fori_loop(part * half_tiles, (part + 1) * half_tiles, block, 0, unroll=4)
+
+    def exchange_start(send, recv, send_sem, recv_sem, at, n, target, near):
         for d in sorted(range(1, n), key=lambda d: (-near(d), d)):
             pltpu.make_async_remote_copy(
-                src_ref=send.at[k],
-                dst_ref=recv.at[k, d - 1],
-                send_sem=send_sem.at[k],
-                recv_sem=recv_sem.at[k],
+                src_ref=send.at[at],
+                dst_ref=recv.at[at + (d - 1,)],
+                send_sem=send_sem.at[at],
+                recv_sem=recv_sem.at[at],
                 device_id=target(d),
                 device_id_type=MESH,
             ).start()
 
-    def exchange_end(send, recv, send_sem, recv_sem, k, n, target):
+    def exchange_end(send, recv, send_sem, recv_sem, at, n, target):
         if n > 1:
             pltpu.make_async_remote_copy(
-                src_ref=recv.at[k],
-                dst_ref=recv.at[k],
-                send_sem=send_sem.at[k],
-                recv_sem=recv_sem.at[k],
+                src_ref=recv.at[at],
+                dst_ref=recv.at[at],
+                send_sem=send_sem.at[at],
+                recv_sem=recv_sem.at[at],
                 device_id=target(1),
                 device_id_type=MESH,
             ).wait()
-        parts = [send[k]] + [recv[k, d - 1] for d in range(1, n)]
+        parts = [send[at]] + [recv[at + (d - 1,)] for d in range(1, n)]
         peak = tree_reduce(jnp.maximum, parts)
         total = tree_reduce(jnp.add, [jnp.exp2(v - peak) for v in parts])
         return peak + jnp.log2(total)
 
-    def spread_rows():
+    def spread_rows(part):
         def block(i, carry):
             u = jnp.broadcast_to(row_out[pl.ds(i, 1), :], (TILE, TILE))
             wide[pl.ds(pl.multiple_of(i * TILE, TILE), TILE), :] = jnp.transpose(u)
             return carry
 
-        lax.fori_loop(0, row_tiles, block, 0, unroll=4)
-
-    def column_partial(k):
+        lax.fori_loop(part * half_tiles, (part + 1) * half_tiles, block, 0, unroll=4)
+
+    def column_partial(part, start):
         def block(i, carry):
             base = pl.multiple_of(i * TILE, TILE)
             out = []
@@ -283,11 +314,9 @@
                 out.append((new, total * jnp.exp2(top - new) + add))
             return tuple(out)
 
-        start = tuple(
-            (jnp.full((8, TILE), LOWEST, jnp.float32), jnp.zeros((8, TILE), jnp.float32))
-            for _ in range(col_tiles)
-        )
-        done = lax.fori_loop(0, row_tiles, block, start)
+        return lax.fori_loop(part * half_tiles, (part + 1) * half_tiles, block, start)
+
+    def column_finish(k, done):
         for j in range(col_tiles):
             level = done[j][0] + jnp.log2(done[j][1])
             peak = jnp.max(level, axis=0, keepdims=True)
@@ -303,35 +332,45 @@
     def wrap(d, n):
         return min(d, n - d)
 
+    row_refs = (row_send, row_recv, rs_sem, rr_sem)
+    col_refs = (col_send, col_recv, cs_sem, cr_sem)
+
+    def row_near(d):
+        return wrap(d, n_proto)
+
+    def col_near(d):
+        return wrap(d // side, side) + wrap(d % side, side)
+
     shifts = None
     for k in range(ITERS):
-        if k > 0:
-            row_partial(lanes(shifts))
-        row_finish(k)
-        exchange_start(
-            row_send, row_recv, rs_sem, rr_sem, k, n_proto, proto_peer, lambda d: wrap(d, n_proto)
-        )
+        for i in range(2):
+            if k > 0:
+                row_partial(shifts, i)
+            else:
+                for n in range(1, PARTS):
+                    score_blocks(n, i * half_rows // mm, (i + 1) * half_rows // mm)
+            row_finish(k, i)
+            exchange_start(*row_refs, (k, i), n_proto, proto_peer, row_near)
         if k == 0:
             for i in range(0, protos, TILE):
                 for j in range(0, depth, TILE):
                     feat_t[i : i + TILE, j : j + TILE] = jnp.transpose(feat[j : j + TILE, i : i + TILE])
-        row_out[...] = -exchange_end(row_send, row_recv, rs_sem, rr_sem, k, n_proto, proto_peer)
-        spread_rows()
-        column_partial(k)
-        exchange_start(
-            col_send,
-            col_recv,
-            cs_sem,
-            cr_sem,
-            k,
-            n_row,
-            row_peer,
-            lambda d: wrap(d // side, side) + wrap(d % side, side),
-        )
-        shifts = log_column - exchange_end(col_send, col_recv, cs_sem, cr_sem, k, n_row, row_peer)
-
-    col_out[...] = shifts * LN2
-    shifts = lanes(shifts)
+        columns = tuple(
+            (jnp.full((8, TILE), LOWEST, jnp.float32), jnp.zeros((8, TILE), jnp.float32))
+            for _ in range(col_tiles)
+        )
+        for i in range(2):
+            row_out[i * half_tiles : (i + 1) * half_tiles, :] = -exchange_end(
+                *row_refs, (k, i), n_proto, proto_peer
+            )
+            spread_rows(i)
+            columns = column_partial(i, columns)
+        column_finish(k, columns)
+        exchange_start(*col_refs, (k,), n_row, row_peer, col_near)
+        potential = log_column - exchange_end(*col_refs, (k,), n_row, row_peer)
+        shifts = lanes(potential)
+
+    col_out[...] = potential * LN2
 
     plan = emb
     far = n_z // 2
@@ -462,15 +501,10 @@
         copy.wait_send()
 
 
-def hand_over(a, b, c, a_out, b_out, c_out, sem):
-    copies = [
-        pltpu.make_async_copy(src, dst, sem.at[i])
-        for i, (src, dst) in enumerate(((a, a_out), (b, b_out), (c, c_out)))
-    ]
-    for copy in copies:
-        copy.start()
-    for copy in copies:
-        copy.wait()
+def hand_over(a, b, c, a_out, b_out, c_out):
+    a_out[...] = a[...]
+    b_out[...] = b[...]
+    c_out[...] = c[...]
 
 
 def solution(mesh):
@@ -509,8 +543,8 @@
                 pltpu.VMEM((protos, depth), bf16),
                 pltpu.VMEM((rows, protos), f32),
                 pltpu.VMEM((rows, TILE), f32),
-                pltpu.VMEM((ITERS, row_tiles, TILE), f32),
-                pltpu.VMEM((ITERS, peers_p, row_tiles, TILE), f32),
+                pltpu.VMEM((ITERS, 2, row_tiles // 2, TILE), f32),
+                pltpu.VMEM((ITERS, 2, peers_p, row_tiles // 2, TILE), f32),
                 pltpu.VMEM((ITERS, col_tiles, TILE), f32),
                 pltpu.VMEM((ITERS, peers_r, col_tiles, TILE), f32),
                 pltpu.VMEM((n_z, 2 * share, rows), bf16),
@@ -518,10 +552,10 @@
                 pltpu.VMEM((2, far, SPLIT, share, rows // SPLIT), bf16),
                 pltpu.VMEM((2, far, SPLIT, share, rows // SPLIT), bf16),
                 dma(()),
-                dma((2, 20)),
-                dma((2, 20)),
-                dma((ITERS,)),
-                dma((ITERS,)),
+                dma((PARTS, 2, 20)),
+                dma((PARTS, 2, 20)),
+                dma((ITERS, 2)),
+                dma((ITERS, 2)),
                 dma((ITERS,)),
                 dma((ITERS,)),
                 dma((n_z, SPLIT)),
@@ -533,14 +567,7 @@
                 collective_id=0, has_side_effects=True, vmem_limit_bytes=56 * 1024 * 1024
             ),
         )(prototypes.T, embeddings, block_mask.T)
-        anywhere = pl.BlockSpec(memory_space=pl.ANY)
-        targets, row_potential, column_potential = pl.pallas_call(
-            hand_over,
-            out_shape=shapes,
-            in_specs=[anywhere] * 3,
-            out_specs=(anywhere,) * 3,
-            scratch_shapes=[dma((3,))],
-        )(*results)
+        targets, row_potential, column_potential = pl.pallas_call(hand_over, out_shape=shapes)(*results)
         return (
             targets.T,
             row_potential.reshape(rows),

time: 113 us -> 103 us (0.912)
  Pallas kernels: 113 us -> 102 us
    pallas_call x1, Pallas kernels: 9.44 us -> 1.69 us  [shards(): pl.pallas_call(hand_over, out_shape=shapes)(*results)]
    pallas_call x1, Pallas kernels: 103 us -> 100 us  [shards(): pl.pallas_call(functools.partial(kernel, (side, n_row, n_proto, log_colum...]
where the time goes in v3:
time: 103 us; the launch traced here: 102 us
  Pallas kernels  102 us (99%)
    pallas_call x1, Pallas kernels, shards(): pl.pallas_call(functools.partial(kernel, (side, n_row, n_proto, log_colum...  100 us

profile of v3, /device:TPU:1, one launch (start us, length us, event | category | flops | bytes accessed | tf_op | source)
XLA Modules:
  0.0 102.5 jit_solution(14187805962621578370)
XLA Ops:
  0.6 100.2 %shard_map.58 = (bf16[64,2048]{1,0:T(8,128)(2,1)}, f32[16,128]{1,0:T(8,128)}, f32[8,128]{1,0:T(8,128)}) custom-call(bf16[64,1024]{1,0:T(8,128)(2,1)} %bitcast.5, bf16[2048,1024]{1,0:T(8,128)(2,1)} %emb_hbm.1, s32[8,16]{1,0:T(8,128)} %bitcast.6), custom_call_target="tpu_custom_call" | custom-call | tf_op jit(solution)/shard_map/pallas_call | solution.py:531
  100.8 1.7 %shard_map.59 = (bf16[64,2048]{1,0:T(8,128)(2,1)}, f32[16,128]{1,0:T(8,128)}, f32[8,128]{1,0:T(8,128)}) custom-call(bf16[64,2048]{1,0:T(8,128)(2,1)} %get-tuple-element.9.a, f32[16,128]{1,0:T(8,128)} %get-tuple-element.10.b, f32[8,128]{1,0:T(8,128)} %get-tuple-element.11.c), custom_call_target="tpu_custom_call" | custom-call | tf_op jit(solution)/shard_map/pallas_call | solution.py:570

commit v4 on v3

--- a/solution.py
+++ b/solution.py
@@ -15,7 +15,7 @@
 LOG2E = 1.4426950408889634
 LN2 = 0.6931471805599453
 SPLIT = 4
-PARTS = 2
+PARTS = 1
 MESH = pl.DeviceIdType.MESH
 
 
@@ -58,6 +58,7 @@
     sr_sem,
     ts_sem,
     tr_sem,
+    hello_sem,
 ):
     side, n_row, n_proto, log_column = cfg
     n_z = n_proto // 2
@@ -79,16 +80,29 @@
     emb_copy = pltpu.make_async_copy(emb_hbm, emb, emb_sem)
     emb_copy.start()
 
+    neighbours = [(r, z * 2 + 1 - c)]
+    if n_row > 1:
+        for move in ((0, 1), (0, -1), (1, 0), (-1, 0)):
+            neighbours.append((row_of(*move), p))
+    up, down = lax.rem(z + 1, n_z), lax.rem(z + n_z - 1, n_z)
+    if n_z > 1:
+        for side_z in (up, down):
+            neighbours.extend([(r, side_z * 2 + c), (r, side_z * 2 + 1 - c)])
     barrier = pltpu.get_barrier_semaphore()
-    for d in range(1, n_row):
-        pl.semaphore_signal(
-            barrier, inc=1, device_id=(lax.rem(r + d, n_row), p), device_id_type=MESH
-        )
-    for d in range(1, n_proto):
-        pl.semaphore_signal(
-            barrier, inc=1, device_id=(r, lax.rem(p + d, n_proto)), device_id_type=MESH
-        )
-    pl.semaphore_wait(barrier, n_row + n_proto - 2)
+    for peer in neighbours:
+        pl.semaphore_signal(barrier, inc=1, device_id=peer, device_id_type=MESH)
+    pl.semaphore_wait(barrier, len(neighbours))
+
+    def hello(i):
+        if n_z // 2 > i + 1:
+            for side_z in (up, down):
+                pl.semaphore_signal(
+                    hello_sem.at[i], inc=1, device_id=(r, side_z * 2 + c), device_id_type=MESH
+                )
+
+    def hello_end(i):
+        if n_z // 2 > i + 1:
+            pl.semaphore_wait(hello_sem.at[i], 2)
 
     half, quarter = slab // 2, slab // 4
     span = protos // PARTS
@@ -186,10 +200,15 @@
 
     for n in range(PARTS):
         gather_stage(0, n)
+    hello(0)
     feat[pl.ds(pl.multiple_of(r * slab, slab), slab), :] = own_ref[...]
     for stage in (1, 2, 3, 4):
         for n in range(PARTS):
             gather_stage(stage, n)
+        if stage < 4:
+            hello_end(stage - 1)
+            if stage < 3:
+                hello(stage)
     gather_stage(5, 0)
     gather_stage(6, 0)
 
@@ -232,12 +251,13 @@
         lax.fori_loop(first, last, block, 0)
 
     blocks = rows // mm
-    score_blocks(0, 0, max(blocks // 4, 1))
-    for n in range(1, PARTS):
-        gather_stage(5, n)
-    score_blocks(0, max(blocks // 4, 1), blocks)
-    for n in range(1, PARTS):
-        gather_stage(6, n)
+    if PARTS > 1:
+        score_blocks(0, 0, max(blocks // 4, 1))
+        for n in range(1, PARTS):
+            gather_stage(5, n)
+        score_blocks(0, max(blocks // 4, 1), blocks)
+        for n in range(1, PARTS):
+            gather_stage(6, n)
 
     group = 64
 
@@ -347,7 +367,7 @@
             if k > 0:
                 row_partial(shifts, i)
             else:
-                for n in range(1, PARTS):
+                for n in range(min(1, PARTS - 1), PARTS):
                     score_blocks(n, i * half_rows // mm, (i + 1) * half_rows // mm)
             row_finish(k, i)
             exchange_start(*row_refs, (k, i), n_proto, proto_peer, row_near)
@@ -562,6 +582,7 @@
                 dma((n_z, SPLIT)),
                 dma((2, far, SPLIT)),
                 dma((2, far, SPLIT)),
+                pltpu.SemaphoreType.REGULAR((3,)),
             ],
             compiler_params=pltpu.CompilerParams(
                 collective_id=0, has_side_effects=True, vmem_limit_bytes=56 * 1024 * 1024

time: 103 us -> 99.4 us (0.965)
  Pallas kernels: 102 us -> 98.7 us
    pallas_call x1, Pallas kernels: 100 us -> 97 us  [shards(): pl.pallas_call(functools.partial(kernel, (side, n_row, n_proto, log_colum...]
where the time goes in v4:
time: 99.4 us; the launch traced here: 99.3 us
  Pallas kernels  98.7 us (99%)
    pallas_call x1, Pallas kernels, shards(): pl.pallas_call(functools.partial(kernel, (side, n_row, n_proto, log_colum...  97 us

profile of v4, /device:TPU:1, one launch (start us, length us, event | category | flops | bytes accessed | tf_op | source)
XLA Modules:
  0.0 99.3 jit_solution(9737985385726906022)
XLA Ops:
  0.6 97.0 %shard_map.58 = (bf16[64,2048]{1,0:T(8,128)(2,1)}, f32[16,128]{1,0:T(8,128)}, f32[8,128]{1,0:T(8,128)}) custom-call(bf16[64,1024]{1,0:T(8,128)(2,1)} %bitcast.5, bf16[2048,1024]{1,0:T(8,128)(2,1)} %emb_hbm.1, s32[8,16]{1,0:T(8,128)} %bitcast.6), custom_call_target="tpu_custom_call" | custom-call | tf_op jit(solution)/shard_map/pallas_call | solution.py:551
  97.6 1.7 %shard_map.59 = (bf16[64,2048]{1,0:T(8,128)(2,1)}, f32[16,128]{1,0:T(8,128)}, f32[8,128]{1,0:T(8,128)}) custom-call(bf16[64,2048]{1,0:T(8,128)(2,1)} %get-tuple-element.9.a, f32[16,128]{1,0:T(8,128)} %get-tuple-element.10.b, f32[8,128]{1,0:T(8,128)} %get-tuple-element.11.c), custom_call_target="tpu_custom_call" | custom-call | tf_op jit(solution)/shard_map/pallas_call | solution.py:591

commit v5 on v4

--- a/solution.py
+++ b/solution.py
@@ -14,7 +14,7 @@
 LOWEST = -1e38
 LOG2E = 1.4426950408889634
 LN2 = 0.6931471805599453
-SPLIT = 4
+SPLIT = 2
 PARTS = 1
 MESH = pl.DeviceIdType.MESH
 
@@ -48,6 +48,7 @@
     tx,
     rx,
     emb_sem,
+    own_sem,
     gs_sem,
     gr_sem,
     rs_sem,
@@ -77,8 +78,6 @@
     def row_of(dy, dx):
         return lax.rem(y + dy + 2 * side, side) * side + lax.rem(x + dx + 2 * side, side)
 
-    emb_copy = pltpu.make_async_copy(emb_hbm, emb, emb_sem)
-    emb_copy.start()
 
     neighbours = [(r, z * 2 + 1 - c)]
     if n_row > 1:
@@ -104,6 +103,10 @@
         if n_z // 2 > i + 1:
             pl.semaphore_wait(hello_sem.at[i], 2)
 
+    own_rows = pl.ds(pl.multiple_of(r * slab, slab), slab)
+    own_copy = pltpu.make_async_copy(own_ref, feat.at[own_rows, :], own_sem)
+    own_copy.start()
+
     half, quarter = slab // 2, slab // 4
     span = protos // PARTS
 
@@ -201,20 +204,23 @@
     for n in range(PARTS):
         gather_stage(0, n)
     hello(0)
-    feat[pl.ds(pl.multiple_of(r * slab, slab), slab), :] = own_ref[...]
+    emb_copy = pltpu.make_async_copy(emb_hbm, emb, emb_sem)
+    emb_copy.start()
     for stage in (1, 2, 3, 4):
         for n in range(PARTS):
             gather_stage(stage, n)
-        if stage < 4:
-            hello_end(stage - 1)
-            if stage < 3:
-                hello(stage)
+        if stage == 3:
+            hello_end(0)
+            hello(1)
     gather_stage(5, 0)
+    hello_end(1)
+    hello(2)
     gather_stage(6, 0)
 
     emb_copy.wait()
-
-    mm = min(512, rows // 2)
+    own_copy.wait()
+
+    mm = min(1024, rows // 2)
 
     def lane_lse(vals):
         peak = tree_reduce(jnp.maximum, vals)
@@ -370,6 +376,8 @@
                 for n in range(min(1, PARTS - 1), PARTS):
                     score_blocks(n, i * half_rows // mm, (i + 1) * half_rows // mm)
             row_finish(k, i)
+            if (k, i) == (0, 0):
+                hello_end(2)
             exchange_start(*row_refs, (k, i), n_proto, proto_peer, row_near)
         if k == 0:
             for i in range(0, protos, TILE):
@@ -552,7 +560,7 @@
             functools.partial(kernel, (side, n_row, n_proto, log_column)),
             out_shape=shapes,
             in_specs=[
-                vmem,
+                pl.BlockSpec(memory_space=pl.ANY),
                 pl.BlockSpec(memory_space=pl.ANY),
                 pl.BlockSpec(memory_space=pltpu.SMEM),
             ],
@@ -571,6 +579,7 @@
                 pltpu.VMEM((n_z, SPLIT, share, rows // SPLIT), bf16),
                 pltpu.VMEM((2, far, SPLIT, share, rows // SPLIT), bf16),
                 pltpu.VMEM((2, far, SPLIT, share, rows // SPLIT), bf16),
+                dma(()),
                 dma(()),
                 dma((PARTS, 2, 20)),
                 dma((PARTS, 2, 20)),

time: 99.4 us -> 99 us (level)
  no operation moved by 1% of the time
where the time goes in v5:
time: 99 us; the launch traced here: 98.9 us
  Pallas kernels  98.2 us (99%)
    pallas_call x1, Pallas kernels, shards(): pl.pallas_call(functools.partial(kernel, (side, n_row, n_proto, log_colum...  96.5 us

profile of v5, /device:TPU:1, one launch (start us, length us, event | category | flops | bytes accessed | tf_op | source)
XLA Modules:
  0.0 98.9 jit_solution(11402935237203636079)
XLA Ops:
  0.6 96.5 %shard_map.58 = (bf16[64,2048]{1,0:T(8,128)(2,1)}, f32[16,128]{1,0:T(8,128)}, f32[8,128]{1,0:T(8,128)}) custom-call(bf16[64,1024]{1,0:T(8,128)(2,1)} %bitcast.5, bf16[2048,1024]{1,0:T(8,128)(2,1)} %emb_hbm.1, s32[8,16]{1,0:T(8,128)} %bitcast.6), custom_call_target="tpu_custom_call" | custom-call | tf_op jit(solution)/shard_map/pallas_call | solution.py:559
  97.2 1.7 %shard_map.59 = (bf16[64,2048]{1,0:T(8,128)(2,1)}, f32[16,128]{1,0:T(8,128)}, f32[8,128]{1,0:T(8,128)}) custom-call(bf16[64,2048]{1,0:T(8,128)(2,1)} %get-tuple-element.9.a, f32[16,128]{1,0:T(8,128)} %get-tuple-element.10.b, f32[8,128]{1,0:T(8,128)} %get-tuple-element.11.c), custom_call_target="tpu_custom_call" | custom-call | tf_op jit(solution)/shard_map/pallas_call | solution.py:600
